TPU v7x, 512 devices: a whole 4x4x16 slice. The times are simulated.
512 devices in a mesh: leaf: 4 (over y), row: 4 (over x), col: 32 (over z, core).
Axes of the slice: x: 4, y: 4, z: 16, core: 2. Of those that a mesh axis runs over, the one named last changes fastest.
Arguments:
- fronts: float32 [4, 8192, 8192], P('leaf', 'row', 'col'), as said below
- row_targets: int32 [4, 8192], P('leaf', 'row'), may hold values from -1 to 8191, as said below
- col_targets: int32 [4, 8192], P('leaf', 'col'), may hold values from -1 to 8191, as said below
Outputs:
- factored: float32 [4, 8192, 8192], P('leaf', 'row', 'col')
- parent: float32 [8192, 8192], P(('leaf', 'row'), 'col')
Inputs may be any that keep to these rules, and one draw needn't show every extreme that they name: `fronts`: each front is symmetric and positive definite; in group g the rows and columns from some index of at least 6272 on are those of the identity. `row_targets`: for each group: -1 on the first 512 indices and on the identity rows of its front, 0 or more elsewhere; the non-negative entries of one group are distinct; among one group's entries in an aligned block of 2048 indices at most 128 lie in any one aligned block of 512 parent rows, and one such parent block, the same for every group and block, receives exactly 128 from each. `col_targets`: -1 exactly where row_targets is -1; every other entry lies in the same aligned block of 256 as its own index, and the entries of one group are distinct.
All inputs are finite; a program needn't handle non-finite values.
Results may differ from a plain program's by a relative error of at most 0.0001.
Values sent between devices are 32-bit elements; how exact they have to be, the bound alone decides.
No kernel may reach another device: no remote copies, remote signals or barrier semaphores. Data moves between devices by JAX's collectives and lax.ppermute only.
A program may use at most 64 MiB of HBM per device.

v0:
```python
import jax
import jax.numpy as jnp
from jax import lax
from jax.sharding import PartitionSpec as P

W = 256
PANELS = 2


def broadcast(array, axis, root):
    mine = lax.axis_index(axis) == root
    return lax.psum(jnp.where(mine, array, jnp.zeros_like(array)), axis)


def pack_rows(values, destinations, payload, peer_count, capacity):
    row_count = values.shape[0]
    hit_table = destinations[:, None] == jnp.arange(peer_count, dtype=jnp.int32)[None, :]
    running = jnp.cumsum(hit_table.astype(jnp.int32), axis=0)
    ranking = jnp.sum(jnp.where(hit_table, running, 0), axis=1) - 1
    slot_ids = jnp.where(
        destinations >= 0, destinations * capacity + ranking, peer_count * capacity
    )
    sources = (
        jnp.full((peer_count * capacity,), row_count, jnp.int32)
        .at[slot_ids]
        .set(jnp.arange(row_count, dtype=jnp.int32), mode="drop")
    )
    padded_values = jnp.concatenate([values, jnp.zeros((1, values.shape[1]), values.dtype)], axis=0)
    padded_payload = jnp.concatenate([payload, jnp.full((1,), -1, jnp.int32)])
    return (
        padded_values[sources].reshape(peer_count, capacity, values.shape[1]),
        padded_payload[sources].reshape(peer_count, capacity),
    )


def place_rows(values, offsets, parent_rows):
    flat_values = values.reshape(-1, values.shape[-1])
    flat_offsets = offsets.reshape(-1)
    selector = (jnp.arange(parent_rows, dtype=jnp.int32)[:, None] == flat_offsets[None, :]).astype(
        jnp.float32
    )
    return jnp.dot(selector, flat_values, precision=lax.Precision.HIGHEST)


def shards(fronts, row_targets, col_targets):
    local_block = fronts[0]
    rows_here, cols_here = local_block.shape
    row_index = lax.axis_index("row")
    col_index = lax.axis_index("col")
    row_ids = row_index * rows_here + jnp.arange(rows_here, dtype=jnp.int32)
    highest = lax.Precision.HIGHEST
    for step_index in range(PANELS):
        first_col = step_index * W
        after_col = first_col + W
        row_root = first_col // rows_here
        col_root = first_col // cols_here
        row_offset = first_col - row_root * rows_here
        col_offset = first_col - col_root * cols_here
        diag_block = broadcast(
            local_block[row_offset : row_offset + W, col_offset : col_offset + W], "row", row_root
        )
        lower_factor = jnp.linalg.cholesky(diag_block)
        solved = jax.scipy.linalg.solve_triangular(lower_factor, local_block.T, lower=True).T
        below_rows = (row_ids >= after_col)[:, None]
        masked = jnp.where(below_rows, solved, 0.0)
        spread = broadcast(masked, "col", col_root)
        shift_rows = col_index * cols_here - row_index * rows_here
        intersection = (shift_rows < rows_here) & (shift_rows + cols_here > 0)
        padded = jnp.pad(spread, ((cols_here, cols_here), (0, 0)))
        col_piece = lax.dynamic_slice_in_dim(padded, shift_rows + cols_here, cols_here, 0)
        col_piece = jnp.where(intersection, col_piece, 0.0)
        across = lax.psum(col_piece, "row")
        inside = ((row_ids >= first_col) & (row_ids < after_col))[:, None]
        diagonal_rows = (
            jnp.zeros((rows_here, W), jnp.float32).at[row_offset : row_offset + W].set(lower_factor)
        )
        column = jnp.where(below_rows, solved, jnp.where(inside, diagonal_rows, 0.0))
        local_block = local_block - jnp.dot(spread, across.T, precision=highest)
        existing = local_block
        chosen = jnp.where(col_index == col_root, column, existing)
        local_block = local_block.at[:, col_offset : col_offset + W].set(chosen)
    local_cols = col_targets[0] - col_index * cols_here
    placer = (local_cols[:, None] == jnp.arange(cols_here, dtype=jnp.int32)[None, :]).astype(
        jnp.float32
    )
    placed = jnp.dot(local_block, placer, precision=highest)
    leaves = lax.axis_size("leaf")
    grid_rows = lax.axis_size("row")
    parent_rows = rows_here // leaves
    capacity = parent_rows // grid_rows
    targets = row_targets[0]
    is_live = targets >= 0
    owners = jnp.where(is_live, targets // parent_rows, -1)
    offsets = jnp.where(is_live, targets % parent_rows, -1)
    outgoing, outgoing_offsets = pack_rows(placed, owners, offsets, leaves * grid_rows, capacity)
    received, received_offsets = (
        lax.all_to_all(outgoing, ("leaf", "row"), split_axis=0, concat_axis=0, tiled=True),
        lax.all_to_all(outgoing_offsets, ("leaf", "row"), split_axis=0, concat_axis=0, tiled=True),
    )
    parent = place_rows(received, received_offsets, parent_rows)
    return (local_block[None], parent)


def solution(mesh):
    placed = (P("leaf", "row", "col"), P("leaf", "row"), P("leaf", "col"))
    return jax.shard_map(
        shards,
        mesh=mesh,
        in_specs=placed,
        out_specs=(P("leaf", "row", "col"), P(("leaf", "row"), "col")),
        check_vma=False,
    )
```

profile of v0, /device:TPU:32, one launch (start us, length us, event | category | flops | bytes accessed | tf_op | source)
XLA Modules:
  0.0 886.7 jit_solution(11399776170223109978)
XLA Ops:
  7.2 1.9 copy.20
  10.7 61.4 %all-reduce.13.cloned.1.call-done = f32[256,256]{0,1:T(8,128)} async-done(((f32[256,256]{0,1:T(8,128)}), f32[256,256]{0,1:T(8,128)}) %all-reduce.13.cloned.1.call-update) | async-done | bytes 262160 | tf_op jit(solution)/shard_map/psum | solution.py:12
  74.2 11.7 %cholesky.130 = f32[128,128]{1,0:T(8,128)S(1)} custom-call(f32[128,128]{1,0:T(8,128)S(1)} %cholesky.194), custom_call_target="Cholesky" | custom-call | tf_op jit(solution)/shard_map/jit(cholesky)/cholesky | solution.py:62
  85.9 9.8 %custom-call.13 = f32[1,128,128]{1,2,0:T(8,128)S(1)} custom-call(f32[1,128,128]{2,1,0:T(8,128)S(1)} %get-tuple-element.133), custom_call_target="InvertDiagBlocksLowerTriangular" | custom-call | tf_op jit(solution)/shard_map/jit(cholesky)/cholesky | solution.py:62
  96.2 11.7 %cholesky.147 = f32[128,128]{1,0:T(8,128)S(1)} custom-call(f32[128,128]{1,0:T(8,128)S(1)} %convolution_subtract_fusion.5), custom_call_target="Cholesky" | custom-call | tf_op jit(solution)/shard_map/jit(cholesky)/cholesky | solution.py:62
  111.2 4.6 while.10
  116.4 19.7 %custom-call.14 = f32[2,128,128]{1,2,0:T(8,128)S(1)} custom-call(f32[2,128,128]{2,1,0:T(8,128)S(1)} %get-tuple-element.82), custom_call_target="InvertDiagBlocksLowerTriangular" | custom-call | tf_op jit(solution)/shard_map/jit(_solve_triangular)/triangular_solve | solution.py:63
  142.5 211.6 %all-reduce.15.cloned.1.call-done = f32[2048,256]{0,1:T(8,128)} async-done(((f32[2048,256]{0,1:T(8,128)}), f32[2048,256]{0,1:T(8,128)}) %all-reduce.15.cloned.1.call-update) | async-done | bytes 2097168 | tf_op jit(solution)/shard_map/psum | solution.py:12
  354.1 1.7 fusion.8
  355.8 4.5 reduce-window.6
  360.8 55.5 %all-reduce.17.cloned.1.call-done = f32[256,256]{0,1:T(8,128)} async-done(((f32[256,256]{0,1:T(8,128)}), f32[256,256]{0,1:T(8,128)}) %all-reduce.17.cloned.1.call-update) | async-done | bytes 262160 | tf_op jit(solution)/shard_map/psum | solution.py:72
  416.3 4.8 fusion.2
  423.2 56.5 %all-reduce.19.cloned.1.call-done = f32[256,256]{0,1:T(8,128)} async-done(((f32[256,256]{0,1:T(8,128)}), f32[256,256]{0,1:T(8,128)}) %all-reduce.19.cloned.1.call-update) | async-done | bytes 262160 | tf_op jit(solution)/shard_map/psum | solution.py:12
  481.8 11.7 %cholesky.164 = f32[128,128]{1,0:T(8,128)S(1)} custom-call(f32[128,128]{1,0:T(8,128)S(1)} %cholesky.197), custom_call_target="Cholesky" | custom-call | tf_op jit(solution)/shard_map/jit(cholesky)/cholesky | solution.py:62
  493.5 9.8 %custom-call.15 = f32[1,128,128]{1,2,0:T(8,128)S(1)} custom-call(f32[1,128,128]{2,1,0:T(8,128)S(1)} %get-tuple-element.131), custom_call_target="InvertDiagBlocksLowerTriangular" | custom-call | tf_op jit(solution)/shard_map/jit(cholesky)/cholesky | solution.py:62
  503.8 11.7 %cholesky.181 = f32[128,128]{1,0:T(8,128)S(1)} custom-call(f32[128,128]{1,0:T(8,128)S(1)} %convolution_subtract_fusion.4), custom_call_target="Cholesky" | custom-call | tf_op jit(solution)/shard_map/jit(cholesky)/cholesky | solution.py:62
  519.3 4.5 while.11
  523.8 20.3 %custom-call.16 = f32[2,128,128]{1,2,0:T(8,128)} custom-call(f32[2,128,128]{2,1,0:T(8,128)S(1)} %get-tuple-element.83), custom_call_target="InvertDiagBlocksLowerTriangular" | custom-call | tf_op jit(solution)/shard_map/jit(_solve_triangular)/triangular_solve | solution.py:63
  544.1 1.9 fusion.4
  551.0 8.0 scatter_custom_fusion
  559.0 204.0 %all-reduce.21.cloned.1.call-done = f32[2048,256]{0,1:T(8,128)} async-done(((f32[2048,256]{0,1:T(8,128)}), f32[2048,256]{0,1:T(8,128)}) %all-reduce.21.cloned.1.call-update) | async-done | bytes 2097168 | tf_op jit(solution)/shard_map/psum | solution.py:12
  763.0 1.7 fusion.9
  764.7 20.5 %gather_fusion = s32[2048]{0:T(1024)} fusion(s32[2049]{0:T(1024)S(1)} %pad_add_fusion, s32[2048]{0:T(1024)S(1)} %fusion.42), kind=kCustom, calls=%fused_computation | custom fusion | bytes 24576 | tf_op jit(solution)/shard_map/gather | solution.py:32
  785.3 5.9 all-to-all-start
  791.2 34.1 %all-reduce.23.cloned.1.call-done = f32[256,256]{0,1:T(8,128)} async-done(((f32[256,256]{0,1:T(8,128)}), f32[256,256]{0,1:T(8,128)}) %all-reduce.23.cloned.1.call-update) | async-done | bytes 262160 | tf_op jit(solution)/shard_map/psum | solution.py:72
  825.2 4.2 fusion.1
  829.5 1.9 fusion.17
  831.6 8.6 gather_fusion.1
  840.1 6.4 all-to-all-start.1
  846.6 1.8 copy.34
  848.4 26.5 %all-to-all-done.1 = f32[16,128,256]{2,1,0:T(8,128)} async-done(((f32[16,128,256]{2,1,0:T(8,128)}), f32[16,128,256]{2,1,0:T(8,128)}, u32[]{:S(2)}, u32[]{:S(2)}) %all-to-all-start.1) | async-done | bytes 2097184 | tf_op jit(solution)/shard_map/all_to_all | solution.py:97
  874.9 4.7 fusion
  (125 shorter events, 33.9 us)
Async XLA Ops:
  7.2 64.9 %all-reduce.13.cloned.1.call-start = ((), (), s32[]{:S(2)}) async-start(), calls=%async_computation.2 | async-start | bytes 524288 | tf_op jit(solution)/shard_map/psum | solution.py:12
  9.1 128.0 %copy-start = (f32[1,2048,256]{1,2,0:T(8,128)}, f32[1,2048,256]{1,2,0:T(8,128)S(1)}, u32[]{:S(2)}) copy-start(f32[1,2048,256]{1,2,0:T(8,128)S(1)} %copy.20) | copy-start | bytes 6291460
  10.0 344.1 %all-reduce.15.cloned.1.call-start = ((), (), s32[]{:S(2)}) async-start(), calls=%async_computation.3 | async-start | bytes 4194304 | tf_op jit(solution)/shard_map/psum | solution.py:12
  10.1 129.2 %copy-start.10 = (pred[2048]{0:T(1024)(128)(4,1)}, pred[2048]{0:T(1024)(128)(4,1)S(1)}, u32[]{:S(2)}) copy-start(pred[2048]{0:T(1024)(128)(4,1)S(1)} %fusion.43) | copy-start | bytes 6148
  115.8 0.6 copy-start.13
  139.2 1.0 copy-start.4
  141.8 0.7 copy-start.8
  141.8 274.5 %copy-start.6 = (f32[256,256]{0,1:T(8,128)S(1)}, f32[256,256]{0,1:T(8,128)}, u32[]{:S(2)}) copy-start(f32[256,256]{0,1:T(8,128)} %get-tuple-element.128) | copy-start | bytes 786436
  141.8 274.5 %all-reduce.17.cloned.1.call-start = ((), (), s32[]{:S(2)}) async-start(), calls=%async_computation.4 | async-start | bytes 524288 | tf_op jit(solution)/shard_map/psum | solution.py:72
  355.8 123.9 %all-reduce.19.cloned.1.call-start = ((), (), s32[]{:S(2)}) async-start(), calls=%async_computation.5 | async-start | bytes 524288 | tf_op jit(solution)/shard_map/psum | solution.py:12
  421.2 97.4 %copy-start.11 = (pred[256]{0:T(512)(128)(4,1)S(1)}, pred[256]{0:T(512)(128)(4,1)}, u32[]{:S(2)}) copy-start(pred[256]{0:T(512)(128)(4,1)} %get-tuple-element.104) | copy-start | bytes 772
  421.9 341.1 %all-reduce.21.cloned.1.call-start = ((), (), s32[]{:S(2)}) async-start(), calls=%async_computation.6 | async-start | bytes 4194304 | tf_op jit(solution)/shard_map/psum | solution.py:12
  423.1 96.2 %copy-start.14 = (s32[2,2]{1,0:T(2,128)S(1)}, s32[2,2]{1,0:T(2,128)}, u32[]{:S(2)}) copy-start(s32[2,2]{1,0:T(2,128)} %copy-done.13) | copy-start | bytes 52
  546.0 1.1 copy-start.7
  546.0 3.1 copy-start.9
  548.2 1.0 copy-start.3
  550.7 274.5 %all-reduce.23.cloned.1.call-start = ((), (), s32[]{:S(2)}) async-start(), calls=%async_computation.7 | async-start | bytes 524288 | tf_op jit(solution)/shard_map/psum | solution.py:72
  764.7 26.4 %copy-start.12 = (s32[1,256]{1,0:T(1,128)S(1)}, s32[1,256]{1,0:T(1,128)}, u32[]{:S(2)}) copy-start(s32[1,256]{1,0:T(1,128)} %param.20) | copy-start | bytes 3076
  764.7 60.5 %copy-start.5 = (f32[256,256]{0,1:T(8,128)S(1)}, f32[256,256]{0,1:T(8,128)}, u32[]{:S(2)}) copy-start(f32[256,256]{0,1:T(8,128)} %get-tuple-element.126) | copy-start | bytes 786436
  785.3 54.9 %all-to-all-start = ((s32[16,1,128]{2,1,0:T(1,128)}), s32[16,1,128]{2,1,0:T(1,128)S(1)}, u32[]{:S(2)}, u32[]{:S(2)}) async-start(s32[16,1,128]{2,1,0:T(1,128)} %bitcast.24), calls=%async_computation | async-start | bytes 16384 | tf_op jit(solution)/shard_map/all_to_all | solution.py:98
  829.5 1.9 copy-start.1
  840.1 6.4 copy-start.2
  840.1 34.7 %all-to-all-start.1 = ((f32[16,128,256]{2,1,0:T(8,128)}), f32[16,128,256]{2,1,0:T(8,128)}, u32[]{:S(2)}, u32[]{:S(2)}) async-start(f32[16,128,256]{2,1,0:T(8,128)} %bitcast.122), calls=%async_computation.1 | async-start | bytes 4194304 | tf_op jit(solution)/shard_map/all_to_all | solution.py:97
Sparse Core Ops, SparseCore 0:
  10.9 61.1 all-reduce.12
  141.9 212.1 all-reduce.14
  357.0 59.3 all-reduce.16
  422.1 57.6 all-reduce.18
  550.9 212.0 all-reduce.20
  765.9 59.3 all-reduce.22
where the time goes:
time: 895 us; the launch traced here: 887 us
  waiting for transfers between devices  650 us (73%)
  other arithmetic  126 us (14%)
  local copies, waits for them, and re-layouts  56.1 us (6%)
  matrix products  23.8 us (3%)
  between operations  17.6 us (2%)
  starting transfers between devices  12.9 us (1%)
    psum x4, waiting for transfers between devices, broadcast(): return lax.psum(jnp.where(mine, array, jnp.zeros_like(array)), axis)  533 us
    psum x2, waiting for transfers between devices, shards(): across = lax.psum(col_piece, 'row')  89.6 us
    another operation x13, other arithmetic, shards(): lower_factor = jnp.linalg.cholesky(diag_block)  68.6 us
    another operation x3, other arithmetic, shards(): jax.scipy.linalg.solve_triangular(lower_factor, local_block.T, lower=True)  40 us
    all_to_all x1, waiting for transfers between devices, shards(): lax.all_to_all(outgoing, ('leaf', 'row'), split_axis=0, concat_axis=0, ti...  26.5 us
    gather x1, local copies, waits for them, and re-layouts, pack_rows(): padded_payload[sources].reshape(peer_count, capacity)  20.5 us
  transfers between devices with their start and end apart: 8, of which 7 were waited for; matrix products, arithmetic and copies ran while one was open for 6% of the time, Pallas kernels for 0%

commit v1 on v0

v1 whole, which is shorter than its diff:
```python
import jax
import jax.numpy as jnp
from jax import lax
from jax.experimental import pallas as pl
from jax.experimental.pallas import tpu as pltpu
from jax.sharding import PartitionSpec as P

W = 256
PIV = 512
NB = 128
HIGHEST = lax.Precision.HIGHEST
GRID = ("row", "col")


def dot_f32(a, b, dims=((1,), (0,))):
    return lax.dot_general(
        a, b, (dims, ((), ())), precision=HIGHEST, preferred_element_type=jnp.float32
    )


def split(x):
    high = x.astype(jnp.bfloat16)
    low = (x - high.astype(jnp.float32)).astype(jnp.bfloat16)
    return high, low


def factor_block(block):
    groups = NB // 8
    sub = lax.broadcasted_iota(jnp.int32, (8, NB), 0)
    lane = lax.broadcasted_iota(jnp.int32, (8, NB), 1)
    mat = [block[8 * i : 8 * i + 8, :] for i in range(groups)]
    inv = [jnp.where(lane == sub + 8 * i, 1.0, 0.0).astype(jnp.float32) for i in range(groups)]
    for j in range(NB):
        g, k = divmod(j, 8)
        cols = [jnp.broadcast_to(mat[i][:, j : j + 1], (8, NB)) for i in range(g, groups)]
        pivot = jnp.broadcast_to(cols[0][k : k + 1, :], (8, NB))
        recip = 1.0 / pivot
        row_m = jnp.broadcast_to(mat[g][k : k + 1, :], (8, NB)) * recip
        row_i = jnp.broadcast_to(inv[g][k : k + 1, :], (8, NB)) * recip
        cols[0] = jnp.where(sub > k, cols[0], 0.0)
        for i in range(g, groups):
            mat[i] = mat[i] - cols[i - g] * row_m
            inv[i] = inv[i] - cols[i - g] * row_i
    upper, lower_inv = [], []
    for i in range(groups):
        on_diag = lane == sub + 8 * i
        diag = jnp.sum(jnp.where(on_diag, mat[i], 0.0), axis=1, keepdims=True)
        scale = 1.0 / jnp.sqrt(diag)
        upper.append(jnp.where(lane >= sub + 8 * i, mat[i] * scale, 0.0))
        lower_inv.append(inv[i] * scale)
    return jnp.concatenate(upper, axis=0), jnp.concatenate(lower_inv, axis=0)


def factor_kernel(place, left, right, mine, z_ref, top_ref, work, low, low_inv):
    work[:, 0:W] = left[...]
    work[:, W:PIV] = right[...]
    low[...] = jnp.zeros_like(low)
    low_inv[...] = jnp.zeros_like(low_inv)
    rows = lax.broadcasted_iota(jnp.int32, (PIV, NB), 0)
    for k in range(PIV // NB):
        at = slice(k * NB, (k + 1) * NB)
        upper, inverse = factor_block(work[at, at])
        column = dot_f32(work[:, at], inverse, ((1,), (1,)))
        column = jnp.where(rows >= (k + 1) * NB, column, 0.0)
        if k + 1 < PIV // NB:
            after = slice((k + 1) * NB, PIV)
            below = column[(k + 1) * NB :, :]
            work[after, after] = work[after, after] - dot_f32(below, below, ((1,), (1,)))
        if k:
            carried = dot_f32(low[at, 0 : k * NB], low_inv[0 : k * NB, 0 : k * NB])
            low_inv[at, 0 : k * NB] = -dot_f32(inverse, carried)
        low_inv[at, at] = inverse
        low[:, at] = column
        low[at, at] = upper.T
    col = place[1]
    own = mine[...]
    solved = dot_f32(low_inv[...], own)
    unit_row = lax.broadcasted_iota(jnp.int32, (PIV, W), 0)
    unit_col = lax.broadcasted_iota(jnp.int32, (PIV, W), 1)
    unit = jnp.where(unit_row == unit_col + col * W, -1.0, 0.0)
    chosen = jnp.where(col < PIV // W, unit, solved)
    z_ref[...] = dot_f32(low_inv[...], chosen, ((0,), (0,)))
    top_ref[0:W, :] = own[0:W, :]
    top_ref[W:PIV, :] = own[W:PIV, :] - dot_f32(low[W:PIV, 0:W], solved[0:W, :])

    @pl.when(col == 0)
    def _():
        top_ref[...] = low[:, 0:W]

    @pl.when(col == 1)
    def _():
        top_ref[...] = low[:, W:PIV]


def update_kernel(place, front, panel, z_ref, top, col_place, slot, out_ref, send_ref, pair):
    row, col = place[0], place[1]
    keep = jnp.where(col < PIV // W, 0.0, 1.0)
    weights = []
    for a in range(4):
        start = pl.multiple_of(((a - row) & 3) * NB, NB)
        weights.append(z_ref[pl.ds(start, NB), :])
    z_all = jnp.concatenate(weights, axis=0)
    for b in range(8):
        at = slice(b * W, (b + 1) * W)
        lhs = jnp.concatenate([panel[8 * a + b] for a in range(4)], axis=0)
        value = front[at, :] * keep - dot_f32(lhs, z_all, ((0,), (0,)))
        out_ref[at, :] = value

    @pl.when(row == 0)
    def _():
        out_ref[0:PIV, :] = top[...]

    for b in range(8):
        at = slice(b * W, (b + 1) * W)
        high, low = split(out_ref[at, :])
        pair[at, 0:W] = jnp.dot(high, col_place[...], preferred_element_type=jnp.float32).astype(jnp.bfloat16)
        pair[at, W : 2 * W] = jnp.dot(low, col_place[...], preferred_element_type=jnp.float32).astype(jnp.bfloat16)
    for b in range(4):
        want = lax.broadcasted_iota(jnp.int32, (512, 2048), 0) + b * 512
        hit = jnp.where(slot[...] == want, 1.0, 0.0).astype(jnp.bfloat16)
        both = jnp.dot(hit, pair[...], preferred_element_type=jnp.float32)
        send_ref[b * 512 : (b + 1) * 512, :] = both[:, 0:W] + both[:, W : 2 * W]


def place_kernel(select, values, out_ref):
    high, low = split(values[...])
    out_ref[...] = jnp.dot(select[...], high, preferred_element_type=jnp.float32) + jnp.dot(
        select[...], low, preferred_element_type=jnp.float32
    )


SMEM = pl.BlockSpec(memory_space=pltpu.SMEM)
VMEM = pl.BlockSpec(memory_space=pltpu.VMEM)
PARAMS = pltpu.CompilerParams(vmem_limit_bytes=56 << 20)


def cost(flops, moved):
    return pl.CostEstimate(flops=flops, bytes_accessed=moved, transcendentals=0)


def shards(fronts, row_targets, col_targets):
    f32 = jnp.float32
    front = fronts[0]
    rows_here, cols_here = front.shape
    row = lax.axis_index("row")
    col = lax.axis_index("col")
    place = jnp.stack([row, col]).astype(jnp.int32)
    head = front[0:PIV, :]

    shares = [
        lax.ppermute(
            head[j * NB : (j + 1) * NB],
            GRID,
            [(8 * r + b, r * 32 + 8 * ((r + j) % 4) + b) for r in range(4) for b in range(8)],
        )
        for j in range(4)
    ]
    share = shares[0] + shares[1] + shares[2] + shares[3]
    panel = lax.all_gather(share, "col")

    piece = lax.all_to_all(head.reshape(4, NB, W), "row", 0, 0, tiled=True)[0]
    piece = jnp.where(col < 2, piece, 0.0)
    first = [lax.ppermute(piece, "col", [(q, q + 8 * j) for q in range(2)]) for j in range(1, 4)]
    piece = piece + (first[0] + first[1]) + first[2]
    second = [
        lax.ppermute(piece, "col", [(8 * a + q, 8 * a + q + 2 * j) for a in range(4) for q in range(2)])
        for j in range(1, 4)
    ]
    piece = piece + (second[0] + second[1]) + second[2]
    half = lax.all_gather(piece, "row", tiled=True)
    other = lax.ppermute(half, "col", [(i, i ^ 1) for i in range(32)])
    even = (col % 2) == 0
    left = jnp.where(even, half, other)
    right = jnp.where(even, other, half)

    spread = [lax.ppermute(head, "row", [(0, j)]) for j in range(1, 4)]
    mine = jnp.where(row == 0, head, spread[0] + spread[1] + spread[2])

    z_all, top = pl.pallas_call(
        factor_kernel,
        out_shape=[jax.ShapeDtypeStruct((PIV, W), f32)] * 2,
        in_specs=[SMEM, VMEM, VMEM, VMEM],
        out_specs=[VMEM, VMEM],
        scratch_shapes=[pltpu.VMEM((PIV, PIV), f32)] * 3,
        compiler_params=PARAMS,
        cost_estimate=cost(40_000_000_000, 4 << 20),
    )(place, left, right, mine)

    local_cols = col_targets[0] - col * cols_here
    col_place = (local_cols[:, None] == jnp.arange(cols_here, dtype=jnp.int32)[None, :]).astype(jnp.bfloat16)
    targets = row_targets[0]
    live = targets >= 0
    owners = jnp.where(live, targets // 512, -1)
    hits = owners[:, None] == jnp.arange(16, dtype=jnp.int32)[None, :]
    index = jnp.arange(rows_here, dtype=jnp.int32)
    before = (index[:, None] > index[None, :]).astype(jnp.bfloat16)
    ranks = jnp.dot(before, hits.astype(jnp.bfloat16), preferred_element_type=f32)
    rank = jnp.sum(jnp.where(hits, ranks, 0.0), axis=1).astype(jnp.int32)
    slot = jnp.where(live, owners * 128 + rank, -1)
    offset = jnp.where(live, targets % 512 + 1, 0)
    digits = jnp.stack([offset // 16, offset % 16], axis=1).astype(jnp.bfloat16)
    at_slot = (index[:, None] == slot[None, :]).astype(jnp.bfloat16)
    found = jnp.dot(at_slot, digits, preferred_element_type=f32)
    offsets = (found[:, 0] * 16.0 + found[:, 1]).astype(jnp.int32) - 1
    offsets_in = lax.all_to_all(offsets.reshape(16, 1, 128), ("leaf", "row"), 0, 0, tiled=True).reshape(-1)
    select = (jnp.arange(512, dtype=jnp.int32)[:, None] == offsets_in[None, :]).astype(jnp.bfloat16)

    out, send = pl.pallas_call(
        update_kernel,
        out_shape=[jax.ShapeDtypeStruct((rows_here, cols_here), f32)] * 2,
        in_specs=[SMEM] + [VMEM] * 6,
        out_specs=[VMEM, VMEM],
        scratch_shapes=[pltpu.VMEM((rows_here, 2 * cols_here), jnp.bfloat16)],
        compiler_params=PARAMS,
        cost_estimate=cost(6_000_000_000, 12 << 20),
    )(place, front, panel, z_all, top, col_place, slot.reshape(1, rows_here))

    received = lax.all_to_all(send.reshape(16, 128, cols_here), ("leaf", "row"), 0, 0, tiled=True)
    parent = pl.pallas_call(
        place_kernel,
        out_shape=jax.ShapeDtypeStruct((512, cols_here), f32),
        in_specs=[VMEM, VMEM],
        out_specs=VMEM,
        compiler_params=PARAMS,
        cost_estimate=cost(1_000_000_000, 5 << 20),
    )(select, received.reshape(2048, cols_here))
    return (out[None], parent)


def solution(mesh):
    placed = (P("leaf", "row", "col"), P("leaf", "row"), P("leaf", "col"))
    return jax.shard_map(
        shards,
        mesh=mesh,
        in_specs=placed,
        out_specs=(P("leaf", "row", "col"), P(("leaf", "row"), "col")),
        check_vma=False,
    )
```

time: 895 us -> 291 us (0.33)
  waiting for transfers between devices: 650 us -> 80.4 us
  other arithmetic: 126 us -> 7.96 us
  Pallas kernels: 0 us -> 96.3 us
  local copies, waits for them, and re-layouts: 56.1 us -> 4.35 us
  starting transfers between devices: 12.9 us -> 59.9 us
  matrix products: 23.8 us -> 4.34 us
  blocking collectives: 0 us -> 17.9 us
    psum x6 -> x0, waiting for transfers between devices: 623 us -> none  [the longest x4 533 us: broadcast(): return lax.psum(jnp.where(mine, array, jnp.zeros_like(array)), axis)]
    another operation x19 -> x3, other arithmetic: 113 us -> 0.77 us  [the longest x1 0.67 us: shards(): place = jnp.stack([row, col]).astype(jnp.int32)]
    pallas_call x0 -> x3, Pallas kernels: none -> 96.3 us  [the longest x1 78.9 us: shards(): pl.pallas_call(factor_kernel, out_shape=[jax.ShapeDtypeStruct((PIV, W), f...]
    ppermute x0 -> x14, starting transfers between devices: none -> 40.9 us  [the longest x4 23.5 us: shards(): lax.ppermute(head[j * NB:(j + 1) * NB], GRID, [(8 * r + b, r * 32 + 8 * (...]
    ppermute x0 -> x14, waiting for transfers between devices: none -> 30.3 us  [the longest x3 18.7 us: shards(): lax.ppermute(piece, 'col', [(8 * a + q, 8 * a + q + 2 * j) for a in range...]
    gather x2 -> x0, local copies, waits for them, and re-layouts: 29.1 us -> none  [the longest x1 20.5 us: pack_rows(): padded_payload[sources].reshape(peer_count, capacity)]
    all_to_all x2 -> x3, waiting for transfers between devices: 26.5 us -> 50.1 us  [the longest x1 32.2 us: shards(): lax.all_to_all(send.reshape(16, 128, cols_here), ('leaf', 'row'), 0, 0, t...]
    all_gather x0 -> x1, blocking collectives: none -> 17.9 us  [shards(): half = lax.all_gather(piece, 'row', tiled=True)]
  transfers between devices with their start and end apart: 8 -> 18, of which waited for: 7 -> 5; matrix products, arithmetic and copies ran while one was open for 6% -> 5% of each run, Pallas kernels for 0% -> 32%
where the time goes in v1:
time: 291 us; the launch traced here: 286 us
  Pallas kernels  96.3 us (33%)
  waiting for transfers between devices  80.4 us (28%)
  starting transfers between devices  59.9 us (21%)
  blocking collectives  17.9 us (6%)
  between operations  14.6 us (5%)
  other arithmetic  7.96 us (3%)
  local copies, waits for them, and re-layouts  4.35 us (1%)
  matrix products  4.34 us (1%)
    pallas_call x1, Pallas kernels, shards(): pl.pallas_call(factor_kernel, out_shape=[jax.ShapeDtypeStruct((PIV, W), f...  78.9 us
    all_to_all x1, waiting for transfers between devices, shards(): lax.all_to_all(send.reshape(16, 128, cols_here), ('leaf', 'row'), 0, 0, t...  32.2 us
    ppermute x4, starting transfers between devices, shards(): lax.ppermute(head[j * NB:(j + 1) * NB], GRID, [(8 * r + b, r * 32 + 8 * (...  23.5 us
    ppermute x3, waiting for transfers between devices, shards(): lax.ppermute(piece, 'col', [(8 * a + q, 8 * a + q + 2 * j) for a in range...  18.7 us
    all_to_all x1, waiting for transfers between devices, shards(): piece = lax.all_to_all(head.reshape(4, NB, W), 'row', 0, 0, tiled=True)[0]  17.9 us
    all_gather x1, blocking collectives, shards(): half = lax.all_gather(piece, 'row', tiled=True)  17.9 us
    pallas_call x1, Pallas kernels, shards(): pl.pallas_call(update_kernel, out_shape=[jax.ShapeDtypeStruct((rows_here,...  13.2 us
    ppermute x4, waiting for transfers between devices, shards(): lax.ppermute(head[j * NB:(j + 1) * NB], GRID, [(8 * r + b, r * 32 + 8 * (...  11.5 us
  transfers between devices with their start and end apart: 18, of which 5 were waited for; matrix products, arithmetic and copies ran while one was open for 5% of the time, Pallas kernels for 32%

profile of v1, /device:TPU:32, one launch (start us, length us, event | category | flops | bytes accessed | tf_op | source)
XLA Modules:
  0.0 285.7 jit_solution(9721805792857929140)
XLA Ops:
  7.2 1.1 slice_bitcast_fusion.2
  8.4 0.7 collective-permute-start
  9.0 11.8 %collective-permute-start.1 = (f32[128,256]{1,0:T(8,128)S(1)}, f32[128,256]{1,0:T(8,128)S(1)}, u32[]{:S(2)}, u32[]{:S(2)}) collective-permute-start(f32[128,256]{1,0:T(8,128)S(1)} %get-tuple-element.14), channel_id=1, source_target_pairs={{0,8},{1,9},{2,10},{3,11},{4,12},{5,13},{6,14},{7,15},{8,48},{9,49... | collective-permute-start | bytes 393224 | tf_op jit(solution)/shard_map/ppermute | solution.py:151
  20.9 9.7 %collective-permute-start.2 = (f32[128,256]{1,0:T(8,128)S(1)}, f32[128,256]{1,0:T(8,128)S(1)}, u32[]{:S(2)}, u32[]{:S(2)}) collective-permute-start(f32[128,256]{1,0:T(8,128)S(1)} %get-tuple-element.15), channel_id=1, source_target_pairs={{0,16},{1,17},{2,18},{3,19},{4,20},{5,21},{6,22},{7,23},{8,56},{9,... | collective-permute-start | bytes 393224 | tf_op jit(solution)/shard_map/ppermute | solution.py:151
  30.6 1.3 collective-permute-start.3
  32.0 9.4 %collective-permute-done.2 = f32[128,256]{1,0:T(8,128)S(1)} collective-permute-done((f32[128,256]{1,0:T(8,128)S(1)}, f32[128,256]{1,0:T(8,128)S(1)}, u32[]{:S(2)}, u32[]{:S(2)}) %collective-permute-start.2) | collective-permute-done | bytes 131104 | tf_op jit(solution)/shard_map/ppermute | solution.py:151
  41.3 2.1 collective-permute-done.3
  43.5 0.7 add_add_fusion.2
  44.2 1.9 slice_bitcast_fusion.4
  46.1 4.5 %collective-permute-start.11 = (f32[512,256]{1,0:T(8,128)S(1)}, f32[512,256]{1,0:T(8,128)S(1)}, u32[]{:S(2)}, u32[]{:S(2)}) collective-permute-start(f32[512,256]{1,0:T(8,128)S(1)} %get-tuple-element.12), channel_id=1, source_target_pairs={{0,32},{1,33},{2,34},{3,35},{4,36},{5,37},{6,38},{7,39},{8,40},{9,... | collective-permute-start | bytes 1572872 | tf_op jit(solution)/shard_map/ppermute | solution.py:176
  50.6 1.3 collective-permute-start.12
  51.9 3.5 %all-to-all-start = ((f32[4,128,256]{2,1,0:T(8,128)}), f32[4,128,256]{2,1,0:T(8,128)S(1)}, u32[]{:S(2)}, u32[]{:S(2)}) async-start(f32[4,128,256]{2,1,0:T(8,128)} %bitcast.8), calls=%async_computation | async-start | bytes 1048576 | tf_op jit(solution)/shard_map/all_to_all | solution.py:161
  55.4 1.5 fusion.5
  57.1 2.9 fusion.1
  60.0 17.9 %all-to-all-done = f32[4,128,256]{2,1,0:T(8,128)S(1)} async-done(((f32[4,128,256]{2,1,0:T(8,128)}), f32[4,128,256]{2,1,0:T(8,128)S(1)}, u32[]{:S(2)}, u32[]{:S(2)}) %all-to-all-start) | async-done | bytes 524320 | tf_op jit(solution)/shard_map/all_to_all | solution.py:161
  77.9 0.7 collective-permute-start.4
  80.6 7.9 %all-to-all-start.1 = ((s32[16,1,128]{2,1,0:T(1,128)}), s32[16,1,128]{2,1,0:T(1,128)S(1)}, u32[]{:S(2)}, u32[]{:S(2)}) async-start(s32[16,1,128]{2,1,0:T(1,128)} %fusion.21), calls=%async_computation.1 | async-start | bytes 16384 | tf_op jit(solution)/shard_map/all_to_all | solution.py:205
  88.5 1.3 collective-permute-start.7
  91.2 18.7 %collective-permute-done.7 = f32[128,256]{1,0:T(8,128)S(1)} collective-permute-done((f32[128,256]{1,0:T(8,128)S(1)}, f32[128,256]{1,0:T(8,128)S(1)}, u32[]{:S(2)}, u32[]{:S(2)}) %collective-permute-start.7) | collective-permute-done | bytes 131104 | tf_op jit(solution)/shard_map/ppermute | solution.py:166
  109.9 4.6 %collective-permute-start.13 = (f32[512,256]{1,0:T(8,128)S(1)}, f32[512,256]{1,0:T(8,128)S(1)}, u32[]{:S(2)}, u32[]{:S(2)}) collective-permute-start(f32[512,256]{1,0:T(8,128)S(1)} %get-tuple-element.12), channel_id=1, source_target_pairs={{0,96},{1,97},{2,98},{3,99},{4,100},{5,101},{6,102},{7,103},{8,104... | collective-permute-start | bytes 1572872 | tf_op jit(solution)/shard_map/ppermute | solution.py:176
  114.6 17.9 %all_gather.11 = f32[512,256]{1,0:T(8,128)S(1)} all-gather(f32[128,256]{1,0:T(8,128)S(1)} %add_add_fusion), channel_id=1, replica_groups=mesh['leaf'=4,'row'=4,'col'=32] {'row'}, dimensions={0}, use_global_device_ids=true | all-gather | bytes 655360 | tf_op jit(solution)/shard_map/all_gather | solution.py:170
  132.5 2.4 collective-permute-start.10
  135.5 0.7 fusion.6.col_place
  136.3 2.0 add_select_fusion.mine
  138.3 1.0 broadcast_select_fusion
  139.3 78.9 %shard_map.50 = (f32[512,256]{1,0:T(8,128)}, f32[512,256]{1,0:T(8,128)}) custom-call(s32[2]{0:T(128)} %pad_add_fusion.place, f32[512,256]{1,0:T(8,128)} %get-tuple-element.19.left, f32[512,256]{1,0:T(8,128)} %get-tuple-element.18.right, f32[512,256]{1,0:T(8,128)} %add_select_fusion.mine), custom_call_target="tpu_custom_call" | custom-call | flops 40000000000 | bytes 4194304 | tf_op jit(solution)/shard_map/pallas_call | solution.py:179
  218.2 13.2 %shard_map.51 = (f32[2048,256]{1,0:T(8,128)}, f32[2048,256]{1,0:T(8,128)}) custom-call(s32[2]{0:T(128)} %pad_add_fusion.place, f32[2048,256]{1,0:T(8,128)} %bitcast.36, f32[32,128,256]{2,1,0:T(8,128)} %bitcast.42, f32[512,256]{1,0:T(8,128)} %get-tuple-element.6.z_ref, f32[512,256]{1,0:T(8,128)} %get-tuple-element.7.top, bf16[256,256]{1,0:T(8,128)(2,1)} %fusion.6.col_place, ...), custom_call_target="tpu_custom_call" | custom-call | flops 6000000000 | bytes 12582912 | tf_op jit(solution)/shard_map/pallas_call | solution.py:208
  231.4 7.6 %all-to-all-start.2 = ((f32[16,128,256]{2,1,0:T(8,128)}), f32[16,128,256]{2,1,0:T(8,128)S(1)}, u32[]{:S(2)}, u32[]{:S(2)}) async-start(f32[16,128,256]{2,1,0:T(8,128)} %bitcast.35), calls=%async_computation.2 | async-start | bytes 4194304 | tf_op jit(solution)/shard_map/all_to_all | solution.py:218
  238.9 1.9 fusion.3.select
  240.9 32.2 %all-to-all-done.2 = f32[16,128,256]{2,1,0:T(8,128)S(1)} async-done(((f32[16,128,256]{2,1,0:T(8,128)}), f32[16,128,256]{2,1,0:T(8,128)S(1)}, u32[]{:S(2)}, u32[]{:S(2)}) %all-to-all-start.2) | async-done | bytes 2097184 | tf_op jit(solution)/shard_map/all_to_all | solution.py:218
  273.1 1.3 copy-done
  274.4 4.3 %shard_map.52 = f32[512,256]{1,0:T(8,128)} custom-call(bf16[512,2048]{1,0:T(8,128)(2,1)} %fusion.3.select, f32[2048,256]{1,0:T(8,128)} %bitcast.34), custom_call_target="tpu_custom_call" | custom-call | flops 1000000000 | bytes 5242880 | tf_op jit(solution)/shard_map/pallas_call | solution.py:219
  (37 shorter events, 4.3 us)
Async XLA Ops:
  7.2 48.2 %copy-start.1 = (s32[1,2048]{1,0:T(1,128)S(1)}, s32[1,2048]{1,0:T(1,128)}, u32[]{:S(2)}) copy-start(s32[1,2048]{1,0:T(1,128)} %param.4) | copy-start | bytes 24580
  7.2 211.0 %all-gather.3.cloned.1.call-start = ((), (), s32[]{:S(2)}) async-start(), calls=%async_computation.3 | async-start | bytes 4325376 | tf_op jit(solution)/shard_map/all_gather | solution.py:159
  8.4 23.6 %collective-permute-start = (f32[128,256]{1,0:T(8,128)S(1)}, f32[128,256]{1,0:T(8,128)S(1)}, u32[]{:S(2)}, u32[]{:S(2)}) collective-permute-start(f32[128,256]{1,0:T(8,128)S(1)} %get-tuple-element.16), channel_id=1, source_target_pairs={{0,0},{1,1},{2,2},{3,3},{4,4},{5,5},{6,6},{7,7},{8,40},{9,41},{10,... | collective-permute-start | bytes 393224 | tf_op jit(solution)/shard_map/ppermute | solution.py:151
  9.0 22.9 %collective-permute-start.1 = (f32[128,256]{1,0:T(8,128)S(1)}, f32[128,256]{1,0:T(8,128)S(1)}, u32[]{:S(2)}, u32[]{:S(2)}) collective-permute-start(f32[128,256]{1,0:T(8,128)S(1)} %get-tuple-element.14), channel_id=1, source_target_pairs={{0,8},{1,9},{2,10},{3,11},{4,12},{5,13},{6,14},{7,15},{8,48},{9,49... | collective-permute-start | bytes 393224 | tf_op jit(solution)/shard_map/ppermute | solution.py:151
  20.9 20.5 %collective-permute-start.2 = (f32[128,256]{1,0:T(8,128)S(1)}, f32[128,256]{1,0:T(8,128)S(1)}, u32[]{:S(2)}, u32[]{:S(2)}) collective-permute-start(f32[128,256]{1,0:T(8,128)S(1)} %get-tuple-element.15), channel_id=1, source_target_pairs={{0,16},{1,17},{2,18},{3,19},{4,20},{5,21},{6,22},{7,23},{8,56},{9,... | collective-permute-start | bytes 393224 | tf_op jit(solution)/shard_map/ppermute | solution.py:151
  30.6 12.9 %collective-permute-start.3 = (f32[128,256]{1,0:T(8,128)S(1)}, f32[128,256]{1,0:T(8,128)S(1)}, u32[]{:S(2)}, u32[]{:S(2)}) collective-permute-start(f32[128,256]{1,0:T(8,128)S(1)} %get-tuple-element.17), channel_id=1, source_target_pairs={{0,24},{1,25},{2,26},{3,27},{4,28},{5,29},{6,30},{7,31},{8,32},{9,... | collective-permute-start | bytes 393224 | tf_op jit(solution)/shard_map/ppermute | solution.py:151
  46.1 90.1 %collective-permute-start.11 = (f32[512,256]{1,0:T(8,128)S(1)}, f32[512,256]{1,0:T(8,128)S(1)}, u32[]{:S(2)}, u32[]{:S(2)}) collective-permute-start(f32[512,256]{1,0:T(8,128)S(1)} %get-tuple-element.12), channel_id=1, source_target_pairs={{0,32},{1,33},{2,34},{3,35},{4,36},{5,37},{6,38},{7,39},{8,40},{9,... | collective-permute-start | bytes 1572872 | tf_op jit(solution)/shard_map/ppermute | solution.py:176
  50.6 85.7 %collective-permute-start.12 = (f32[512,256]{1,0:T(8,128)S(1)}, f32[512,256]{1,0:T(8,128)S(1)}, u32[]{:S(2)}, u32[]{:S(2)}) collective-permute-start(f32[512,256]{1,0:T(8,128)S(1)} %get-tuple-element.12), channel_id=1, source_target_pairs={{0,64},{1,65},{2,66},{3,67},{4,68},{5,69},{6,70},{7,71},{8,72},{9,... | collective-permute-start | bytes 1572872 | tf_op jit(solution)/shard_map/ppermute | solution.py:176
  51.9 26.0 %all-to-all-start = ((f32[4,128,256]{2,1,0:T(8,128)}), f32[4,128,256]{2,1,0:T(8,128)S(1)}, u32[]{:S(2)}, u32[]{:S(2)}) async-start(f32[4,128,256]{2,1,0:T(8,128)} %bitcast.8), calls=%async_computation | async-start | bytes 1048576 | tf_op jit(solution)/shard_map/all_to_all | solution.py:161
  56.9 34.3 %copy-start.3 = (s32[1,256]{1,0:T(1,128)S(1)}, s32[1,256]{1,0:T(1,128)}, u32[]{:S(2)}) copy-start(s32[1,256]{1,0:T(1,128)} %param.5) | copy-start | bytes 3076
  57.1 81.2 %copy-start.2 = (s32[1,2048]{1,0:T(1,128)}, s32[1,2048]{1,0:T(1,128)S(1)}, u32[]{:S(2)}) copy-start(s32[1,2048]{1,0:T(1,128)S(1)} %compare_select_fusion.9.slot) | copy-start | bytes 24580
  77.9 10.6 %collective-permute-start.4 = (f32[128,256]{1,0:T(8,128)S(1)}, f32[128,256]{1,0:T(8,128)S(1)}, u32[]{:S(2)}, u32[]{:S(2)}) collective-permute-start(f32[128,256]{1,0:T(8,128)S(1)} %fusion.7), channel_id=1, source_target_pairs={{0,8},{1,9},{32,40},{33,41},{64,72},{65,73},{96,104},{97,105},{128... | collective-permute-start | bytes 393224 | tf_op jit(solution)/shard_map/ppermute | solution.py:163
  78.6 9.9 %collective-permute-start.5 = (f32[128,256]{1,0:T(8,128)S(1)}, f32[128,256]{1,0:T(8,128)S(1)}, u32[]{:S(2)}, u32[]{:S(2)}) collective-permute-start(f32[128,256]{1,0:T(8,128)S(1)} %fusion.7), channel_id=1, source_target_pairs={{0,16},{1,17},{32,48},{33,49},{64,80},{65,81},{96,112},{97,113},{1... | collective-permute-start | bytes 393224 | tf_op jit(solution)/shard_map/ppermute | solution.py:163
  79.3 9.2 %collective-permute-start.6 = (f32[128,256]{1,0:T(8,128)S(1)}, f32[128,256]{1,0:T(8,128)S(1)}, u32[]{:S(2)}, u32[]{:S(2)}) collective-permute-start(f32[128,256]{1,0:T(8,128)S(1)} %fusion.7), channel_id=1, source_target_pairs={{0,24},{1,25},{32,56},{33,57},{64,88},{65,89},{96,120},{97,121},{1... | collective-permute-start | bytes 393224 | tf_op jit(solution)/shard_map/ppermute | solution.py:163
  80.6 150.8 %all-to-all-start.1 = ((s32[16,1,128]{2,1,0:T(1,128)}), s32[16,1,128]{2,1,0:T(1,128)S(1)}, u32[]{:S(2)}, u32[]{:S(2)}) async-start(s32[16,1,128]{2,1,0:T(1,128)} %fusion.21), calls=%async_computation.1 | async-start | bytes 16384 | tf_op jit(solution)/shard_map/all_to_all | solution.py:205
  88.5 21.4 %collective-permute-start.7 = (f32[128,256]{1,0:T(8,128)S(1)}, f32[128,256]{1,0:T(8,128)S(1)}, u32[]{:S(2)}, u32[]{:S(2)}) collective-permute-start(f32[128,256]{1,0:T(8,128)S(1)} %add_add_fusion.1), channel_id=1, source_target_pairs={{0,2},{1,3},{8,10},{9,11},{16,18},{17,19},{24,26},{25,27},{32,34},... | collective-permute-start | bytes 393224 | tf_op jit(solution)/shard_map/ppermute | solution.py:166
  89.8 24.7 %collective-permute-start.8 = (f32[128,256]{1,0:T(8,128)S(1)}, f32[128,256]{1,0:T(8,128)S(1)}, u32[]{:S(2)}, u32[]{:S(2)}) collective-permute-start(f32[128,256]{1,0:T(8,128)S(1)} %add_add_fusion.1), channel_id=1, source_target_pairs={{0,4},{1,5},{8,12},{9,13},{16,20},{17,21},{24,28},{25,29},{32,36},... | collective-permute-start | bytes 393224 | tf_op jit(solution)/shard_map/ppermute | solution.py:166
  90.5 24.0 %collective-permute-start.9 = (f32[128,256]{1,0:T(8,128)S(1)}, f32[128,256]{1,0:T(8,128)S(1)}, u32[]{:S(2)}, u32[]{:S(2)}) collective-permute-start(f32[128,256]{1,0:T(8,128)S(1)} %add_add_fusion.1), channel_id=1, source_target_pairs={{0,6},{1,7},{8,14},{9,15},{16,22},{17,23},{24,30},{25,31},{32,38},... | collective-permute-start | bytes 393224 | tf_op jit(solution)/shard_map/ppermute | solution.py:166
  109.9 26.3 %collective-permute-start.13 = (f32[512,256]{1,0:T(8,128)S(1)}, f32[512,256]{1,0:T(8,128)S(1)}, u32[]{:S(2)}, u32[]{:S(2)}) collective-permute-start(f32[512,256]{1,0:T(8,128)S(1)} %get-tuple-element.12), channel_id=1, source_target_pairs={{0,96},{1,97},{2,98},{3,99},{4,100},{5,101},{6,102},{7,103},{8,104... | collective-permute-start | bytes 1572872 | tf_op jit(solution)/shard_map/ppermute | solution.py:176
  132.5 5.8 %collective-permute-start.10 = (f32[512,256]{1,0:T(8,128)S(1)}, f32[512,256]{1,0:T(8,128)S(1)}, u32[]{:S(2)}, u32[]{:S(2)}) collective-permute-start(f32[512,256]{1,0:T(8,128)S(1)} %all_gather.11), channel_id=1, source_target_pairs={{0,1},{1,0},{2,3},{3,2},{4,5},{5,4},{6,7},{7,6},{8,9},{9,8},{10,11... | collective-permute-start | bytes 1572872 | tf_op jit(solution)/shard_map/ppermute | solution.py:171
  231.4 41.7 %all-to-all-start.2 = ((f32[16,128,256]{2,1,0:T(8,128)}), f32[16,128,256]{2,1,0:T(8,128)S(1)}, u32[]{:S(2)}, u32[]{:S(2)}) async-start(f32[16,128,256]{2,1,0:T(8,128)} %bitcast.35), calls=%async_computation.2 | async-start | bytes 4194304 | tf_op jit(solution)/shard_map/all_to_all | solution.py:218
  273.1 1.3 copy-start
Sparse Core Ops, SparseCore 0:
  44.3 77.2 all-gather.2
